TPU v7x, 128 devices: a whole 4x4x4 slice. The times are simulated.
128 devices in a mesh: dp: 16 (over x, y), expert: 8 (over z, core).
Axes of the slice: x: 4, y: 4, z: 4, core: 2. Of those that a mesh axis runs over, the one named last changes fastest.
Arguments:
- tokens: bfloat16 [2048, 6144], P('dp'), may hold values from -6 to 6
- routes: int32 [2048, 2], P('dp'), may hold values from 0 to 7, all different within a row; in each aligned block of 128 rows (0 to 127, 128 to 255, ...) at most 64 rows name the same one
- gates: float32 [2048, 2], P('dp'), may hold values from 0.1 to 1
- capacity: int32 [8], replicated, may hold values from 32 to 64, as said below
- w_gate: bfloat16 [8, 6144, 8192], P('expert', None, 'dp'), may hold values from -0.078125 to 0.078125
- w_up: bfloat16 [8, 6144, 8192], P('expert', None, 'dp'), may hold values from -0.078125 to 0.078125
- w_down: bfloat16 [8, 8192, 6144], P('expert', 'dp'), may hold values from -0.0625 to 0.0625
Outputs:
- mixed: bfloat16 [2048, 6144], P('dp', 'expert')
Inputs may be any that keep to these rules, and one draw needn't show every extreme that they name: `routes`: each token names two different experts. Within the 128 tokens of one index of dp no expert is named by more than 64 tokens, and in some shards one expert is named by exactly 64. Some expert's capacity is exactly 64.
All inputs are finite; a program needn't handle non-finite values.
Results may differ from a plain program's by a relative error of at most 0.015.
Values may be sent and summed in bfloat16 or wider, within the bound.
No kernel may reach another device: no remote copies, remote signals or barrier semaphores. Data moves between devices by JAX's collectives and lax.ppermute only.
A program may use at most 128 MiB of HBM per device.

v0:
```python
import jax
import jax.numpy as jnp
from jax import lax
from jax.sharding import PartitionSpec as P


def on_device(tokens, routes, gates, capacity, w_gate, w_up, w_down):
    owner_index = lax.axis_index("expert")
    group_size = lax.axis_size("expert")
    local_rows = tokens.shape[0]
    num_experts = group_size * w_gate.shape[0]
    slot_count = 4 * local_rows // num_experts
    matched = routes == owner_index
    member = jnp.any(matched, axis=-1).astype(jnp.int32)
    weight = jnp.sum(jnp.where(matched, gates, 0.0), axis=-1)
    position = jnp.cumsum(member) - member
    limit_value = jnp.sum(
        jnp.where(jnp.arange(num_experts, dtype=jnp.int32) == owner_index, capacity, 0)
    )
    retained = (member == 1) & (position < limit_value)
    slot_ids = jnp.arange(slot_count, dtype=jnp.int32)
    selector = (retained[None, :] & (position[None, :] == slot_ids[:, None])).astype(jnp.bfloat16)
    slot_rows = jnp.dot(selector, tokens, preferred_element_type=jnp.float32).astype(jnp.bfloat16)
    gate_panel = w_gate[0]
    up_panel = w_up[0]
    down_panel = w_down[0]
    block_rows = lax.all_gather(slot_rows, "dp", axis=0, tiled=True)
    gate_value = jnp.dot(block_rows, gate_panel, preferred_element_type=jnp.float32)
    up_value = jnp.dot(block_rows, up_panel, preferred_element_type=jnp.float32)
    hidden = (jax.nn.silu(gate_value) * up_value).astype(jnp.bfloat16)
    partial_value = jnp.dot(hidden, down_panel, preferred_element_type=jnp.float32)
    returned = lax.psum_scatter(
        partial_value.astype(jnp.bfloat16), "dp", scatter_dimension=0, tiled=True
    ).astype(jnp.float32)
    placed = jnp.einsum(
        "ct,cd->td", selector.astype(jnp.float32), returned, precision=lax.Precision.HIGHEST
    )
    weighted = weight[:, None] * placed
    summed = lax.psum(weighted.astype(jnp.bfloat16), "expert").astype(jnp.float32)
    feature_width = summed.shape[1] // group_size
    result = lax.dynamic_slice_in_dim(summed, owner_index * feature_width, feature_width, 1)
    return result.astype(jnp.bfloat16)


def solution(mesh):
    in_specs = (
        P("dp", None),
        P("dp", None),
        P("dp", None),
        P(),
        P("expert", None, "dp"),
        P("expert", None, "dp"),
        P("expert", "dp", None),
    )
    out_specs = P("dp", "expert")
    return jax.shard_map(
        on_device, mesh=mesh, in_specs=in_specs, out_specs=out_specs, check_vma=False
    )
```

profile of v0, /device:TPU:0, one launch (start us, length us, event | category | flops | bytes accessed | tf_op | source)
XLA Modules:
  0.0 303.3 jit_solution(16822140769576966833)
XLA Ops:
  6.5 0.0 copy-start
  6.5 0.0 all-gather.2.cloned.1.call-start
  6.5 0.8 fusion.16
  7.4 0.1 copy.9
  7.5 0.2 reduce-window.7
  7.7 0.1 reduce
  7.8 1.3 fusion.15
  9.1 0.7 compare_and_fusion
  9.7 0.0 copy-done
  9.7 1.3 convolution_convert_fusion.1
  11.0 0.0 all-gather.2.cloned.1.call-update
  11.0 0.0 reduce-scatter.2.cloned.1.call-start
  11.1 92.2 %all-gather.2.cloned.1.call-done = bf16[1024,6144]{1,0:T(8,128)(2,1)} async-done(((bf16[64,6144]{1,0:T(8,128)(2,1)}), bf16[1024,6144]{1,0:T(8,128)(2,1)}) %all-gather.2.cloned.1.call-update) | async-done | bytes 12582928 | tf_op jit(solution)/shard_map/all_gather | solution.py:27
  103.3 0.0 copy-start.3
  103.3 11.6 %fusion.2 = f32[1024,512]{1,0:T(8,128)S(1)} fusion(bf16[1024,6144]{1,0:T(8,128)(2,1)} %all-gather.2.cloned.1.call-done, bf16[1,6144,512]{2,1,0:T(8,128)(2,1)} %param.12), kind=kOutput, calls=%fused_computation.5 | convolution fusion | flops 6442450944 | bytes 20971520 | tf_op jit(solution)/shard_map/dot_general | solution.py:29
  114.9 0.0 copy-done.3
  114.9 0.0 copy-start.4
  114.9 9.0 %multiply_convert_fusion = bf16[1024,512]{1,0:T(8,128)(2,1)S(1)} fusion(f32[1024,512]{1,0:T(8,128)S(1)} %fusion.2, bf16[1024,6144]{1,0:T(8,128)(2,1)S(1)} %copy-done.3, bf16[1,6144,512]{2,1,0:T(8,128)(2,1)} %param.11), kind=kOutput, calls=%fused_computation.9 | convolution fusion | flops 6445596672 | bytes 22020096 | tf_op jit(solution)/shard_map/dot_general | solution.py:28
  124.0 0.0 copy-done.4
  124.0 9.6 %convolution_convert_fusion = bf16[1024,6144]{1,0:T(8,128)(2,1)} fusion(bf16[1024,512]{1,0:T(8,128)(2,1)S(1)} %multiply_convert_fusion, bf16[1,512,6144]{2,1,0:T(8,128)(2,1)S(1)} %copy-done.4), kind=kOutput, calls=%fused_computation | convolution fusion | flops 6448742400 | bytes 19922944 | tf_op jit(solution)/shard_map/dot_general | solution.py:31
  133.6 0.0 copy-start.1
  133.6 0.0 copy-start.2
  133.6 0.0 reduce-scatter.2.cloned.1.call-update
  133.6 0.0 all-reduce.2.cloned.1.call-start
  133.6 0.6 copy-done.1
  134.2 0.0 copy-done.2
  134.3 94.4 %reduce-scatter.2.cloned.1.call-done = bf16[64,6144]{1,0:T(8,128)(2,1)} async-done(((bf16[1024,6144]{1,0:T(8,128)(2,1)}), bf16[64,6144]{1,0:T(8,128)(2,1)}) %reduce-scatter.2.cloned.1.call-update) | async-done | bytes 786448 | tf_op jit(solution)/shard_map/reduce_scatter | solution.py:32
  228.7 2.9 fusion
  231.6 0.0 all-reduce.2.cloned.1.call-update
  231.6 63.5 %all-reduce.2.cloned.1.call-done = bf16[128,6144]{1,0:T(8,128)(2,1)} async-done(((bf16[128,6144]{1,0:T(8,128)(2,1)}), bf16[128,6144]{1,0:T(8,128)(2,1)}) %all-reduce.2.cloned.1.call-update) | async-done | bytes 1572880 | tf_op jit(solution)/shard_map/psum | solution.py:39
  295.1 1.6 convert_convert_fusion
  (3 shorter events, 0.0 us)
Async XLA Ops:
  6.5 3.2 %copy-start = (bf16[128,6144]{1,0:T(8,128)(2,1)S(1)}, bf16[128,6144]{1,0:T(8,128)(2,1)}, u32[]{:S(2)}) copy-start(bf16[128,6144]{1,0:T(8,128)(2,1)} %param.7) | copy-start | bytes 4718596
  6.5 96.8 %all-gather.2.cloned.1.call-start = ((), (), s32[]{:S(2)}) async-start(), calls=%async_computation.1 | async-start | bytes 13369344 | tf_op jit(solution)/shard_map/all_gather | solution.py:27
  11.0 217.6 %reduce-scatter.2.cloned.1.call-start = ((), (), s32[]{:S(2)}) async-start(), calls=%async_computation.2 | async-start | bytes 13369344 | tf_op jit(solution)/shard_map/reduce_scatter | solution.py:32
  103.3 11.6 %copy-start.3 = (bf16[1024,6144]{1,0:T(8,128)(2,1)S(1)}, bf16[1024,6144]{1,0:T(8,128)(2,1)}, u32[]{:S(2)}) copy-start(bf16[1024,6144]{1,0:T(8,128)(2,1)} %all-gather.2.cloned.1.call-done) | copy-start | bytes 37748740
  114.9 9.1 %copy-start.4 = (bf16[1,512,6144]{2,1,0:T(8,128)(2,1)S(1)}, bf16[1,512,6144]{2,1,0:T(8,128)(2,1)}, u32[]{:S(2)}) copy-start(bf16[1,512,6144]{2,1,0:T(8,128)(2,1)} %param.13) | copy-start | bytes 18874372
  133.6 0.7 copy-start.1
  133.6 0.7 copy-start.2
  133.6 161.5 %all-reduce.2.cloned.1.call-start = ((), (), s32[]{:S(2)}) async-start(), calls=%async_computation.3 | async-start | bytes 3145728 | tf_op jit(solution)/shard_map/psum | solution.py:39
Sparse Core Ops, SparseCore 0:
  11.2 92.1 all-gather.1
  133.7 94.9 reduce-scatter.1
  231.7 63.3 all-reduce.1
where the time goes:
time: 304 us; the launch traced here: 303 us
  waiting for transfers between devices  250 us (82%)
  matrix products  34.4 us (11%)
  between operations  13.2 us (4%)
  other arithmetic  4.69 us (2%)
    reduce_scatter x1, waiting for transfers between devices, on_device(): lax.psum_scatter(partial_value.astype(jnp.bfloat16), 'dp', scatter_dimens...  94.4 us
    all_gather x1, waiting for transfers between devices, on_device(): block_rows = lax.all_gather(slot_rows, 'dp', axis=0, tiled=True)  92.2 us
    psum x1, waiting for transfers between devices, on_device(): lax.psum(weighted.astype(jnp.bfloat16), 'expert').astype(jnp.float32)  63.5 us
    dot_general x1, matrix products, on_device(): up_value = jnp.dot(block_rows, up_panel, preferred_element_type=jnp.float32)  11.6 us
    dot_general x1, matrix products, on_device(): jnp.dot(hidden, down_panel, preferred_element_type=jnp.float32)  9.56 us
    dot_general x1, matrix products, on_device(): jnp.dot(block_rows, gate_panel, preferred_element_type=jnp.float32)  9.04 us
  transfers between devices with their start and end apart: 3, of which 3 were waited for; matrix products, arithmetic and copies ran while one was open for 0% of the time, Pallas kernels for 0%

commit v1 on v0

--- a/solution.py
+++ b/solution.py
@@ -24,7 +24,9 @@
     gate_panel = w_gate[0]
     up_panel = w_up[0]
     down_panel = w_down[0]
-    block_rows = lax.all_gather(slot_rows, "dp", axis=0, tiled=True)
+    block_rows = jnp.concatenate(
+        lax.all_to_all(jnp.stack([slot_rows] * lax.axis_size("dp")), "dp", 0, 0), axis=0
+    )
     gate_value = jnp.dot(block_rows, gate_panel, preferred_element_type=jnp.float32)
     up_value = jnp.dot(block_rows, up_panel, preferred_element_type=jnp.float32)
     hidden = (jax.nn.silu(gate_value) * up_value).astype(jnp.bfloat16)

time: 304 us -> 363 us (1.19)
  blocking collectives: 0 us -> 149 us
  waiting for transfers between devices: 250 us -> 157 us
  local copies, waits for them, and re-layouts: 0.75 us -> 6.89 us
    all_to_all x0 -> x1, blocking collectives: none -> 149 us  [on_device(): lax.all_to_all(jnp.stack([slot_rows] * lax.axis_size('dp')), 'dp', 0, 0)]
    all_gather x1 -> x0, waiting for transfers between devices: 92.2 us -> none  [on_device(): block_rows = lax.all_gather(slot_rows, 'dp', axis=0, tiled=True)]
    another operation x0 -> x1, local copies, waits for them, and re-layouts: none -> 6.14 us  [on_device(): jnp.stack([slot_rows] * lax.axis_size('dp'))]
  transfers between devices with their start and end apart: 3 -> 2, of which waited for: 3 -> 2; matrix products, arithmetic and copies ran while one was open for 0% -> 0% of each run, Pallas kernels for 0% -> 0%
where the time goes in v1:
time: 363 us
  waiting for transfers between devices  157 us (43%)
  blocking collectives  149 us (41%)
  matrix products  31.3 us (9%)
  between operations  13.5 us (4%)
  local copies, waits for them, and re-layouts  6.89 us (2%)
  other arithmetic  4.69 us (1%)
    all_to_all x1, blocking collectives, on_device(): lax.all_to_all(jnp.stack([slot_rows] * lax.axis_size('dp')), 'dp', 0, 0)  149 us
    reduce_scatter x1, waiting for transfers between devices, on_device(): lax.psum_scatter(partial_value.astype(jnp.bfloat16), 'dp', scatter_dimens...  93.9 us
    psum x1, waiting for transfers between devices, on_device(): lax.psum(weighted.astype(jnp.bfloat16), 'expert').astype(jnp.float32)  63.5 us
    dot_general x1, matrix products, on_device(): up_value = jnp.dot(block_rows, up_panel, preferred_element_type=jnp.float32)  9.96 us
    dot_general x1, matrix products, on_device(): jnp.dot(hidden, down_panel, preferred_element_type=jnp.float32)  9.65 us
    dot_general x1, matrix products, on_device(): jnp.dot(block_rows, gate_panel, preferred_element_type=jnp.float32)  8.37 us
  transfers between devices with their start and end apart: 2, of which 2 were waited for; matrix products, arithmetic and copies ran while one was open for 0% of the time, Pallas kernels for 0%

profile of v1, /device:TPU:0, one launch (start us, length us, event | category | flops | bytes accessed | tf_op | source)
XLA Modules:
  0.0 363.2 jit_solution(7021934161952952420)
XLA Ops:
  6.5 0.0 copy-start
  6.5 0.0 reduce-scatter.2.cloned.1.call-start
  6.5 0.8 fusion.16
  7.4 0.1 copy.9
  7.5 0.2 reduce-window.7
  7.7 0.1 reduce
  7.8 1.3 fusion.15
  9.1 0.7 compare_and_fusion
  9.7 0.0 copy-done
  9.7 0.4 convolution_convert_fusion.1
  10.1 6.1 %stack.2 = bf16[16,64,6144]{2,1,0:T(8,128)(2,1)} broadcast(bf16[64,6144]{1,0:T(8,128)(2,1)S(1)} %convolution_convert_fusion.1), dimensions={1,2} | broadcast | bytes 13369344 | tf_op jit(solution)/shard_map/stack | solution.py:28
  16.2 0.0 slice-start
  16.2 0.0 slice-start.2
  16.2 149.4 %all_to_all.5 = bf16[16,64,6144]{2,1,0:T(8,128)(2,1)S(1)} all-to-all(bf16[16,64,6144]{2,1,0:T(8,128)(2,1)} %stack.2), channel_id=1, replica_groups=mesh['dp'=16,'expert'=8] {'dp'}, dimensions={0} | all-to-all | bytes 25165824 | tf_op jit(solution)/shard_map/all_to_all | solution.py:28
  165.6 0.0 slice-start.1
  165.6 0.0 slice-start.3
  165.6 10.0 %fusion.2 = f32[1024,512]{1,0:T(8,128)} fusion(bf16[1024,6144]{1,0:T(8,128)(2,1)S(1)} %bitcast.19, bf16[1,6144,512]{2,1,0:T(8,128)(2,1)} %param.12), kind=kOutput, calls=%fused_computation.5 | convolution fusion | flops 6442450944 | bytes 20971520 | tf_op jit(solution)/shard_map/dot_general | solution.py:31
  175.6 0.0 slice-done
  175.6 0.0 slice-done.1
  175.6 8.4 %multiply_convert_fusion = bf16[1024,512]{1,0:T(8,128)(2,1)S(1)} fusion(f32[1024,512]{1,0:T(8,128)} %fusion.2, bf16[1024,6144]{1,0:T(8,128)(2,1)S(1)} %bitcast.20, bf16[1,6144,512]{2,1,0:T(8,128)(2,1)S(1)} %bitcast.22), kind=kOutput, calls=%fused_computation.9 | convolution fusion | flops 6445596672 | bytes 22020096 | tf_op jit(solution)/shard_map/dot_general | solution.py:30
  184.0 0.0 slice-done.2
  184.0 0.0 slice-done.3
  184.0 9.7 %convolution_convert_fusion = bf16[1024,6144]{1,0:T(8,128)(2,1)} fusion(bf16[1024,512]{1,0:T(8,128)(2,1)S(1)} %multiply_convert_fusion, bf16[1,512,6144]{2,1,0:T(8,128)(2,1)S(1)} %bitcast.24), kind=kOutput, calls=%fused_computation | convolution fusion | flops 6448742400 | bytes 19922944 | tf_op jit(solution)/shard_map/dot_general | solution.py:33
  193.7 0.0 copy-start.1
  193.7 0.0 copy-start.2
  193.7 0.0 reduce-scatter.2.cloned.1.call-update
  193.7 0.0 all-reduce.2.cloned.1.call-start
  193.7 0.6 copy-done.1
  194.3 0.0 copy-done.2
  194.4 93.9 %reduce-scatter.2.cloned.1.call-done = bf16[64,6144]{1,0:T(8,128)(2,1)} async-done(((bf16[1024,6144]{1,0:T(8,128)(2,1)}), bf16[64,6144]{1,0:T(8,128)(2,1)}) %reduce-scatter.2.cloned.1.call-update) | async-done | bytes 786448 | tf_op jit(solution)/shard_map/reduce_scatter | solution.py:34
  288.3 2.9 fusion
  291.2 0.0 all-reduce.2.cloned.1.call-update
  291.3 63.5 %all-reduce.2.cloned.1.call-done = bf16[128,6144]{1,0:T(8,128)(2,1)} async-done(((bf16[128,6144]{1,0:T(8,128)(2,1)}), bf16[128,6144]{1,0:T(8,128)(2,1)}) %all-reduce.2.cloned.1.call-update) | async-done | bytes 1572880 | tf_op jit(solution)/shard_map/psum | solution.py:41
  354.8 1.6 convert_convert_fusion
  (5 shorter events, 0.0 us)
Async XLA Ops:
  6.5 3.2 copy-start
  6.5 281.8 %reduce-scatter.2.cloned.1.call-start = ((), (), s32[]{:S(2)}) async-start(), calls=%async_computation.2 | async-start | bytes 13369344 | tf_op jit(solution)/shard_map/reduce_scatter | solution.py:34
  16.2 159.4 %slice-start = ((s8[6291456]{0:T(1024)(128)(4,1)}), s8[4194304]{0:T(1024)(128)(4,1)S(1)}, s32[]{:S(2)}) async-start(s8[6291456]{0:T(1024)(128)(4,1)} %bitcast.21), calls=%async_computation.4 | async-start | bytes 8388608
  16.2 167.7 %slice-start.2 = ((s8[6291456]{0:T(1024)(128)(4,1)}), s8[4194304]{0:T(1024)(128)(4,1)S(1)}, s32[]{:S(2)}) async-start(s8[6291456]{0:T(1024)(128)(4,1)} %bitcast.23), calls=%async_computation.6 | async-start | bytes 8388608
  165.6 10.0 %slice-start.1 = ((s8[6291456]{0:T(1024)(128)(4,1)}), s8[2097152]{0:T(1024)(128)(4,1)S(1)}, s32[]{:S(2)}) async-start(s8[6291456]{0:T(1024)(128)(4,1)} %bitcast.21), calls=%async_computation.5 | async-start | bytes 4194304
  165.6 18.4 %slice-start.3 = ((s8[6291456]{0:T(1024)(128)(4,1)}), s8[2097152]{0:T(1024)(128)(4,1)S(1)}, s32[]{:S(2)}) async-start(s8[6291456]{0:T(1024)(128)(4,1)} %bitcast.23), calls=%async_computation.7 | async-start | bytes 4194304
  193.7 0.7 copy-start.1
  193.7 0.7 copy-start.2
  193.7 161.1 %all-reduce.2.cloned.1.call-start = ((), (), s32[]{:S(2)}) async-start(), calls=%async_computation.3 | async-start | bytes 3145728 | tf_op jit(solution)/shard_map/psum | solution.py:41
Sparse Core Ops, SparseCore 0:
  193.8 94.4 reduce-scatter.1
  291.4 63.3 all-reduce.1
